TPU v7x, 128 devices: a whole 4x4x4 slice. The times are simulated.
128 devices in a mesh: dp: 16 (over y, z), ctx: 8 (over x, core).
Axes of the slice: x: 4, y: 4, z: 4, core: 2. Of those that a mesh axis runs over, the one named last changes fastest.
Arguments:
- state_input: bfloat16 [32768, 4096], P(('dp', 'ctx')), may hold values from -6 to 6
- gate_values: bfloat16 [32768, 4096], P(('dp', 'ctx')), may hold values from -6 to 6
- input_matrix: bfloat16 [32768, 512], P(('dp', 'ctx')), may hold values from -1.2 to 1.2
- readout_matrix: bfloat16 [32768, 512], P(('dp', 'ctx')), may hold values from -1.1953125 to 1.1953125
- step_unbiased: float32 [32768, 64], P(('dp', 'ctx')), may hold values from -3 to 2560
- step_bias: float32 [64], replicated, may hold values from -1 to 0.5
- decay_rate_log: float32 [64], replicated
- skip_coefficients: float32 [64], replicated, may hold values from 3 to 10
- norm_gain: float32 [4096], replicated, may hold values from 0.1 to 8
- adapter_down: bfloat16 [64, 4096], replicated, may hold values from -0.09375 to 0.09375
- adapter_up: bfloat16 [64, 2048], replicated, may hold values from -0.75 to 0.75
- projection_weight: bfloat16 [2048, 4096], P(('dp', 'ctx')), may hold values from -0.09375 to 0.09375
- output_cotangent: bfloat16 [32768, 2048], P(('dp', 'ctx')), may hold values from -30 to 30
Outputs:
- input_gradient: bfloat16 [32768, 4096], P(('dp', 'ctx'))
- adapter_down_gradient: float32 [64, 4096], P(None, ('dp', 'ctx'))
- adapter_up_gradient: float32 [64, 2048], P(None, ('dp', 'ctx'))
All inputs are finite; a program needn't handle non-finite values.
Results may differ from a plain program's by a relative error of at most 0.009.
Values may be sent and summed in bfloat16 or wider, within the bound.
A program may use at most 192 MiB of HBM per device.

v0:
```python
import jax
import jax.numpy as jnp
from jax import lax
from jax.sharding import PartitionSpec as P

H = 64
P_SIZE = 64
N = 128
G = 4
Q = 256
INNER_CHANNELS = 4096
EPS_NORM = 1e-05
CLIP_EPSILON = 1e-06
ADAPTER_SCALE = 2.0


def entering(value, axis, join, neutral):
    count, mine = (lax.axis_size(axis), lax.axis_index(axis))
    pieces = jax.tree.map(lambda part: lax.all_gather(part, axis), value)
    running = jax.tree.map(
        lambda part, zero: jnp.full_like(part, 0) + jnp.asarray(zero, part.dtype), value, neutral
    )

    def lap(position, running):
        longer = join(running, jax.tree.map(lambda part: part[position], pieces))
        return jax.tree.map(lambda new, old: jnp.where(position < mine, new, old), longer, running)

    return lax.fori_loop(0, count - 1, lap, running)


def carried_in(value, axis, join, neutral):
    count = lax.axis_size(axis)
    place = lax.axis_index(axis)
    ahead = count - 1 - place
    gathered = jax.tree.map(
        lambda a, kind: lax.all_gather(a.astype(kind), axis), value, (jnp.bfloat16, jnp.bfloat16)
    )
    state = jax.tree.map(lambda a, e: jnp.zeros_like(a) + jnp.asarray(e, a.dtype), value, neutral)

    def one(lap, state):
        source = count - 1 - lap
        return join(
            state,
            jax.tree.map(
                lambda a, own: lax.dynamic_index_in_dim(a, source, 0, False).astype(own.dtype),
                gathered,
                value,
            ),
        )

    return lax.fori_loop(0, ahead, one, state)


def combine(earlier, later):
    return (earlier[0] * later[0], earlier[1] * later[0][:, None, None] + later[1])


def spread_heads(grouped, lead):
    wide = jnp.broadcast_to(grouped[..., :, None, :], lead + (G, H // G, grouped.shape[-1]))
    return wide.reshape(lead + (H, grouped.shape[-1]))


def on_device(
    state_input,
    gate_values,
    input_matrix,
    readout_matrix,
    step_unbiased,
    step_bias,
    decay_rate_log,
    skip_coefficients,
    norm_gain,
    adapter_down,
    adapter_up,
    projection_weight,
    output_cotangent,
):
    row_count = state_input.shape[0]
    block_count = row_count // Q
    group_width = INNER_CHANNELS // G
    per_group = H // G
    step_size = jax.nn.softplus(step_unbiased + step_bias[None, :])
    cum_decay = jnp.cumsum(
        (-jnp.exp(decay_rate_log)[None, :] * step_size).reshape(block_count, Q, H), axis=1
    )
    block_total = cum_decay[:, -1, :]
    x_heads = state_input.reshape(row_count, H, P_SIZE)
    xdt_all = (
        (x_heads * step_size[:, :, None]).astype(jnp.bfloat16).reshape(block_count, Q, H, P_SIZE)
    )
    b_blocks = input_matrix.reshape(block_count, Q, G, N)
    c_blocks = readout_matrix.reshape(block_count, Q, G, N)
    inner_prod = jnp.einsum(
        "kign,kjgn->kgij", c_blocks, b_blocks, preferred_element_type=jnp.float32
    )
    inner_prod = jnp.broadcast_to(
        inner_prod[:, :, None], (block_count, G, per_group, Q, Q)
    ).reshape(block_count, H, Q, Q)
    cum_heads = jnp.swapaxes(cum_decay, 1, 2)
    gap_logs = cum_heads[:, :, :, None] - cum_heads[:, :, None, :]
    causal = (
        lax.broadcasted_iota(jnp.int32, (Q, Q), 0) >= lax.broadcasted_iota(jnp.int32, (Q, Q), 1)
    )[None, None]
    scores = (
        inner_prod * jnp.where(causal, jnp.exp(jnp.where(causal, gap_logs, 0.0)), 0.0)
    ).astype(jnp.bfloat16)
    intra_part = jnp.einsum("khij,kjhp->kihp", scores, xdt_all, preferred_element_type=jnp.float32)
    b_heads = spread_heads(b_blocks, (block_count, Q))
    b_weighted = (jnp.exp(block_total[:, None, :] - cum_decay)[..., None] * b_heads).astype(
        jnp.bfloat16
    )
    block_state = jnp.einsum(
        "kjhn,kjhp->khnp", b_weighted, xdt_all, preferred_element_type=jnp.float32
    )

    def step_forward(run_state, block_item):
        decay_log, fresh_state = block_item
        return (jnp.exp(decay_log)[:, None, None] * run_state + fresh_state, run_state)

    zero_state = jnp.zeros((H, N, P_SIZE), jnp.float32)
    device_state, local_in = lax.scan(step_forward, zero_state, (block_total, block_state))
    device_decay = jnp.exp(jnp.sum(block_total, axis=0))
    identity = (jnp.ones((H,), jnp.float32), zero_state)
    unused_decay, incoming = entering((device_decay, device_state), "ctx", combine, identity)
    before = jnp.cumsum(block_total, axis=0) - block_total
    state_in = local_in + jnp.exp(before)[:, :, None, None] * incoming[None]
    incoming_bf = state_in.astype(jnp.bfloat16).reshape(block_count, G, per_group, N, P_SIZE)
    inter_part = jnp.einsum(
        "kign,kgmnp->kigmp", c_blocks, incoming_bf, preferred_element_type=jnp.float32
    ).reshape(block_count, Q, H, P_SIZE)
    ssd_heads = (intra_part + jnp.exp(cum_decay)[..., None] * inter_part).reshape(
        row_count, H, P_SIZE
    ) + skip_coefficients[None, :, None] * x_heads
    silu_z = jax.nn.silu(gate_values.astype(jnp.float32))
    weight_groups = norm_gain.reshape(G, group_width)
    gated = (ssd_heads.reshape(row_count, INNER_CHANNELS) * silu_z).reshape(
        row_count, G, group_width
    )
    rstd = lax.rsqrt(jnp.mean(gated * gated, axis=-1, keepdims=True) + EPS_NORM)
    normalized = (
        (gated * rstd * weight_groups).reshape(row_count, INNER_CHANNELS).astype(jnp.bfloat16)
    )
    down_product = lax.dot_general(
        normalized, adapter_down, (((1,), (1,)), ((), ())), preferred_element_type=jnp.float32
    ).astype(jnp.bfloat16)
    upper_gradient = lax.dot_general(
        output_cotangent, adapter_up, (((1,), (1,)), ((), ())), preferred_element_type=jnp.float32
    ).astype(jnp.bfloat16)
    down_portion = ADAPTER_SCALE * lax.dot_general(
        upper_gradient, normalized, (((0,), (0,)), ((), ())), preferred_element_type=jnp.float32
    )
    up_portion = ADAPTER_SCALE * lax.dot_general(
        down_product, output_cotangent, (((0,), (0,)), ((), ())), preferred_element_type=jnp.float32
    )
    adapter_initial = ADAPTER_SCALE * jnp.dot(
        upper_gradient, adapter_down, preferred_element_type=jnp.float32
    )
    combined_weight = lax.all_gather(projection_weight, ("dp", "ctx"), axis=0, tiled=True)
    normed_gradient = adapter_initial + jnp.dot(
        output_cotangent, combined_weight, preferred_element_type=jnp.float32
    )
    weighted_grad = normed_gradient.reshape(row_count, G, group_width) * weight_groups
    d_gated = rstd * weighted_grad - gated * (rstd * rstd * rstd) * jnp.mean(
        gated * weighted_grad, axis=-1, keepdims=True
    )
    d_ssd = d_gated.reshape(row_count, INNER_CHANNELS) * silu_z
    d_ssd_bf = d_ssd.reshape(block_count, Q, H, P_SIZE).astype(jnp.bfloat16)
    intra_back = jnp.einsum("khij,kihp->kjhp", scores, d_ssd_bf, preferred_element_type=jnp.float32)
    c_heads = spread_heads(c_blocks, (block_count, Q))
    c_weighted = (jnp.exp(cum_decay)[..., None] * c_heads).astype(jnp.bfloat16)
    block_grad = jnp.einsum(
        "kihn,kihp->khnp", c_weighted, d_ssd_bf, preferred_element_type=jnp.float32
    )

    def step_backward(grad_state, block_item):
        decay_log, fresh_state = block_item
        return (jnp.exp(decay_log)[:, None, None] * grad_state + fresh_state, grad_state)

    device_grad, local_out = lax.scan(
        step_backward, zero_state, (block_total, block_grad), reverse=True
    )
    unused_back, outgoing = carried_in((device_decay, device_grad), "ctx", combine, identity)
    after_sum = jnp.flip(jnp.cumsum(jnp.flip(block_total, axis=0), axis=0), axis=0) - block_total
    grad_in = local_out + jnp.exp(after_sum)[:, :, None, None] * outgoing[None]
    outgoing_bf = grad_in.astype(jnp.bfloat16)
    cross_part = jnp.einsum(
        "kjhn,khnp->kjhp", b_weighted, outgoing_bf, preferred_element_type=jnp.float32
    )
    grad_heads = step_size[:, :, None] * (intra_back + cross_part).reshape(
        row_count, H, P_SIZE
    ) + skip_coefficients[None, :, None] * d_ssd.reshape(row_count, H, P_SIZE)
    input_gradient = grad_heads.reshape(row_count, INNER_CHANNELS).astype(jnp.bfloat16)
    down_total, up_total = lax.psum((down_portion, up_portion), ("dp", "ctx"))
    down_root_mean = jnp.sqrt(jnp.mean(down_total * down_total) + CLIP_EPSILON)
    up_root_mean = jnp.sqrt(jnp.mean(up_total * up_total) + CLIP_EPSILON)
    device_total = lax.axis_size(("dp", "ctx"))
    position = lax.axis_index(("dp", "ctx"))
    width_a = down_total.shape[1] // device_total
    width_b = up_total.shape[1] // device_total
    down_fraction = lax.dynamic_slice_in_dim(down_total, position * width_a, width_a, 1)
    up_fraction = lax.dynamic_slice_in_dim(up_total, position * width_b, width_b, 1)
    adapter_down_gradient = down_fraction / jnp.maximum(1.0, down_root_mean)
    adapter_up_gradient = up_fraction / jnp.maximum(1.0, up_root_mean)
    return (input_gradient, adapter_down_gradient, adapter_up_gradient)


def solution(mesh):
    placed = (
        P(("dp", "ctx"), None),
        P(("dp", "ctx"), None),
        P(("dp", "ctx"), None),
        P(("dp", "ctx"), None),
        P(("dp", "ctx"), None),
        P(),
        P(),
        P(),
        P(),
        P(),
        P(),
        P(("dp", "ctx"), None),
        P(("dp", "ctx"), None),
    )
    return jax.shard_map(
        on_device,
        mesh=mesh,
        in_specs=placed,
        out_specs=(P(("dp", "ctx"), None), P(None, ("dp", "ctx")), P(None, ("dp", "ctx"))),
        check_vma=False,
    )
```

profile of v0, /device:TPU:0, one launch (start us, length us, event | category | flops | bytes accessed | tf_op | source)
XLA Modules:
  0.0 570.3 jit_solution(756266060873161029)
XLA Ops:
  14.8 3.0 copy.131
  17.7 3.8 fusion.3
  28.1 5.6 fusion.1
  33.8 11.3 %all-gather = f32[8,1,64]{2,1,0:T(1,128)} all-gather(f32[1,1,64]{2,1,0:T(1,128)S(1)} %copy-done.22), channel_id=2, replica_groups=mesh['dp'=16,'ctx'=8] {'ctx'}, dimensions={0}, use_global_device_ids=true | all-gather | bytes 2304 | tf_op jit(solution)/shard_map/all_gather | solution.py:19
  46.1 67.2 %all-gather.10.cloned.1.call-done = f32[512,128,64]{1,2,0:T(8,128)} async-done(((f32[64,128,64]{1,2,0:T(8,128)}), f32[512,128,64]{1,2,0:T(8,128)}) %all-gather.10.cloned.1.call-update) | async-done | bytes 16777232 | tf_op jit(solution)/shard_map/all_gather | solution.py:19
  113.3 80.0 %while.19 = (s32[]{:T(128)}, f32[64,128,64]{2,1,0:T(8,128)}, s32[]{:T(128)}, f32[8,64]{1,0:T(8,128)}, f32[8,64,128,64]{2,3,1,0:T(8,128)}, /*index=5*/s32[]{:T(128)}, s32[]{:T(128)}) while((s32[]{:T(128)}, f32[64,128,64]{2,1,0:T(8,128)}, s32[]{:T(128)}, f32[8,64]{1,0:T(8,128)}, f32[8,64,128,64]{2,3,1,0:T(8,128)}, ...), condition=%wide.region_3.4_spmd.clone, body=%wide.region_2.3_spmd.clone.sunk | while | flops 2097156 | bytes 14680945 | solution.py:28
  118.5 4.9 fusion.43
  125.1 2.8 copy.195
  128.6 6.1 %fusion.43 = f32[64,128,64]{2,1,0:T(8,128)} fusion(f32[1,64,128,64]{3,2,1,0:T(8,128)} %copy.195, f32[64,128,64]{2,1,0:T(8,128)} %get-tuple-element.418, f32[64]{0:T(128)S(1)} %dynamic-slice_bitcast_fusion.2, pred[]{:T(512)S(6)} %compare.3, pred[]{:T(512)S(6)} %lt.51), kind=kLoop, calls=%fused_computation.4.clone.1 | loop fusion | flops 2097152 | bytes 6291714 | tf_op jit(solution)/shard_map/while/body/eval_jaxpr/jit(_where)/select_n | solution.py:26
  139.9 6.1 %fusion.43 = f32[64,128,64]{2,1,0:T(8,128)} fusion(f32[1,64,128,64]{3,2,1,0:T(8,128)} %copy.195, f32[64,128,64]{2,1,0:T(8,128)} %get-tuple-element.418, f32[64]{0:T(128)S(1)} %dynamic-slice_bitcast_fusion.2, pred[]{:T(512)S(6)} %compare.3, pred[]{:T(512)S(6)} %lt.51), kind=kLoop, calls=%fused_computation.4.clone.1 | loop fusion | flops 2097152 | bytes 6291714 | tf_op jit(solution)/shard_map/while/body/eval_jaxpr/jit(_where)/select_n | solution.py:26
  151.2 6.3 %fusion.43 = f32[64,128,64]{2,1,0:T(8,128)} fusion(f32[1,64,128,64]{3,2,1,0:T(8,128)} %copy.195, f32[64,128,64]{2,1,0:T(8,128)} %get-tuple-element.418, f32[64]{0:T(128)S(1)} %dynamic-slice_bitcast_fusion.2, pred[]{:T(512)S(6)} %compare.3, pred[]{:T(512)S(6)} %lt.51), kind=kLoop, calls=%fused_computation.4.clone.1 | loop fusion | flops 2097152 | bytes 6291714 | tf_op jit(solution)/shard_map/while/body/eval_jaxpr/jit(_where)/select_n | solution.py:26
  162.8 6.1 %fusion.43 = f32[64,128,64]{2,1,0:T(8,128)} fusion(f32[1,64,128,64]{3,2,1,0:T(8,128)} %copy.195, f32[64,128,64]{2,1,0:T(8,128)} %get-tuple-element.418, f32[64]{0:T(128)S(1)} %dynamic-slice_bitcast_fusion.2, pred[]{:T(512)S(6)} %compare.3, pred[]{:T(512)S(6)} %lt.51), kind=kLoop, calls=%fused_computation.4.clone.1 | loop fusion | flops 2097152 | bytes 6291714 | tf_op jit(solution)/shard_map/while/body/eval_jaxpr/jit(_where)/select_n | solution.py:26
  174.7 6.8 %fusion.43 = f32[64,128,64]{2,1,0:T(8,128)} fusion(f32[1,64,128,64]{3,2,1,0:T(8,128)} %copy.195, f32[64,128,64]{2,1,0:T(8,128)} %get-tuple-element.418, f32[64]{0:T(128)S(1)} %dynamic-slice_bitcast_fusion.2, pred[]{:T(512)S(6)} %compare.3, pred[]{:T(512)S(6)} %lt.51), kind=kLoop, calls=%fused_computation.4.clone.1 | loop fusion | flops 2097152 | bytes 6291714 | tf_op jit(solution)/shard_map/while/body/eval_jaxpr/jit(_where)/select_n | solution.py:26
  183.3 2.8 copy.195
  186.8 6.5 %fusion.43 = f32[64,128,64]{2,1,0:T(8,128)} fusion(f32[1,64,128,64]{3,2,1,0:T(8,128)} %copy.195, f32[64,128,64]{2,1,0:T(8,128)} %get-tuple-element.418, f32[64]{0:T(128)S(1)} %dynamic-slice_bitcast_fusion.2, pred[]{:T(512)S(6)} %compare.3, pred[]{:T(512)S(6)} %lt.51), kind=kLoop, calls=%fused_computation.4.clone.1 | loop fusion | flops 2097152 | bytes 6291714 | tf_op jit(solution)/shard_map/while/body/eval_jaxpr/jit(_where)/select_n | solution.py:26
  193.4 2.9 multiply_convert_fusion.2
  196.3 2.9 fusion.15
  199.2 8.2 %fusion.8 = f32[1,256,64,64]{1,3,2,0:T(8,128)} fusion(f32[4,16,64,256]{3,2,1,0:T(8,128)} %fusion.15, bf16[64,256,256]{2,1,0:T(8,128)(2,1)S(1)} %copy-done.1, f32[256,64]{0,1:T(8,128)S(1)} %copy.139, f32[256,64,64]{0,2,1:T(8,128)} %bitcast.133, f32[256,64]{0,1:T(8,128)S(1)} %get-tuple-element.338), kind=kOutput, calls=%fused_computation.22 | convolution fusion | flops 541065216 | bytes 21102592 | tf_op jit(solution)/shard_map/khij,kjhp->kihp/dot_general | solution.py:107
  207.3 5.8 %copy.145 = f32[256,4096]{1,0:T(8,128)} copy(f32[256,4096]{0,1:T(8,128)} %bitcast.141) | data formatting | bytes 8388608 | tf_op jit(solution)/shard_map/reshape | solution.py:131
  213.1 6.2 %add_multiply_fusion = f32[256,4096]{1,0:T(8,128)} fusion(f32[256,4096]{1,0:T(8,128)} %copy.145, f32[4096]{0:T(1024)S(1)} %mul.324, bf16[256,4096]{1,0:T(8,128)(2,1)} %param.18, bf16[256,4096]{1,0:T(8,128)(2,1)S(1)} %copy-done.8), kind=kLoop, calls=%fused_computation.29 | loop fusion | flops 9437184 | bytes 12599296 | tf_op jit(solution)/shard_map/mul | solution.py:136
  219.4 6.0 %reshape.335 = f32[256,4,1024]{2,1,0:T(4,128)} reshape(f32[256,4096]{1,0:T(8,128)} %add_multiply_fusion) | data formatting | bytes 8388608 | tf_op jit(solution)/shard_map/reshape | solution.py:136
  225.4 8.2 %fusion.19 = f32[256,4096]{1,0:T(8,128)S(1)} fusion(bf16[256,2048]{1,0:T(8,128)(2,1)S(1)} %copy-done, bf16[2048,4096]{1,0:T(8,128)(2,1)} %all-gather.8.cloned.1.call-done), kind=kOutput, calls=%fused_computation.71 | convolution fusion | flops 4294967296 | bytes 22020096 | tf_op jit(solution)/shard_map/dot_general | solution.py:159
  236.3 6.0 %reshape.336 = f32[256,4,1024]{2,1,0:T(4,128)} reshape(f32[256,4096]{1,0:T(8,128)} %fusion.4) | data formatting | bytes 8388608 | tf_op jit(solution)/shard_map/reshape | solution.py:162
  242.3 4.8 multiply_reduce_fusion.1
  247.7 5.8 %copy.175 = f32[32,8,4,1024]{3,1,2,0:T(8,128)} copy(f32[32,8,4,1024]{3,2,1,0:T(4,128)S(1)} %bitcast.142) | data formatting | bytes 8388608
  254.4 5.8 %copy.174 = f32[32,8,4,1024]{3,1,2,0:T(8,128)} copy(f32[32,8,4,1024]{3,2,1,0:T(4,128)S(1)} %bitcast.143) | data formatting | bytes 8388608
  261.0 4.2 copy.173
  265.2 6.4 %fusion.18 = (bf16[256,4096]{1,0:T(8,128)(2,1)}, f32[256,4096]{1,0:T(8,128)}, bf16[256,4096]{1,0:T(8,128)(2,1)S(1)}) fusion(bf16[256,4096]{1,0:T(8,128)(2,1)} %param.18, f32[256,4096]{1,0:T(8,128)S(1)} %bitcast.137, f32[256,4096]{1,0:T(8,128)S(1)} %copy-done.4, f32[256,4096]{1,0:T(8,128)} %bitcast.138, f32[256,4096]{1,0:T(8,128)S(1)} %bitcast.139, ...), kind=kLoop, calls=%fused_computation.70 | loop fusion | flops 15728640 | bytes 31473664 | tf_op jit(solution)/shard_map/convert_element_type | solution.py:167
  273.0 3.1 convolution_multiply_fusion.2
  276.3 3.8 fusion.2
  280.1 3.3 copy.151
  283.4 4.2 add_convert_fusion.1
  289.9 5.7 copy.156
  295.6 9.0 %all-gather.3 = bf16[8,1,64]{2,1,0:T(2,128)(2,1)S(1)} all-gather(bf16[1,1,64]{2,1,0:T(2,128)(2,1)S(1)} %copy-done.21), channel_id=5, replica_groups=mesh['dp'=16,'ctx'=8] {'ctx'}, dimensions={0}, use_global_device_ids=true | all-gather | bytes 1152 | tf_op jit(solution)/shard_map/all_gather | solution.py:36
  304.5 7.0 %fusion.20 = f32[64,64,256]{2,1,0:T(8,128)} fusion(bf16[256,64,64]{0,2,1:T(8,128)(2,1)S(1)} %bitcast.136, bf16[64,256,256]{2,1,0:T(8,128)(2,1)} %fusion.1), kind=kOutput, calls=%fused_computation.72 | convolution fusion | flops 536870912 | bytes 14680064 | tf_op jit(solution)/shard_map/khij,kihp->kjhp/dot_general | solution.py:168
  311.5 115.6 %all-reduce.3.cloned.1.call-done = (f32[64,4096]{1,0:T(8,128)}, f32[64,2048]{1,0:T(8,128)}) async-done(((f32[64,4096]{1,0:T(8,128)}, f32[64,2048]{1,0:T(8,128)}), (f32[64,4096]{1,0:T(8,128)}, f32[64,2048]{1,0:T(8,128)})) %all-reduce.3.cloned.1.call-update) | async-done | bytes 1572880 | tf_op jit(solution)/shard_map/psum | solution.py:193
  435.4 41.6 %all-gather.12.cloned.1.call-done = bf16[512,128,64]{1,2,0:T(8,128)(2,1)} async-done(((bf16[64,128,64]{1,2,0:T(8,128)(2,1)}), bf16[512,128,64]{1,2,0:T(8,128)(2,1)}) %all-gather.12.cloned.1.call-update) | async-done | bytes 8388624 | tf_op jit(solution)/shard_map/all_gather | solution.py:36
  479.5 62.9 %while.18 = (s32[]{:T(128)}, f32[64,128,64]{2,1,0:T(8,128)}, s32[]{:T(128)}, bf16[8,64]{1,0:T(8,128)(2,1)S(1)}, bf16[8,64,128,64]{2,3,1,0:T(8,128)(2,1)}, /*index=5*/s32[]{:T(128)}, s32[]{:T(128)}, s32[]{:T(128)}, s32[]{:T(128)}) while((s32[]{:T(128)}, f32[64,128,64]{2,1,0:T(8,128)}, s32[]{:T(128)}, bf16[8,64]{1,0:T(8,128)(2,1)S(1)}, ...), condition=%wide.region_7.8_spmd, body=%wide.region_6.7_spmd.sunk | while | flops 1572934 | bytes 9437979 | solution.py:51
  483.8 4.7 convert_add_fusion.2
  492.8 4.7 convert_add_fusion.2
  501.8 4.7 convert_add_fusion.2
  510.7 4.7 convert_add_fusion.2
  519.7 4.7 convert_add_fusion.2
  528.7 4.7 convert_add_fusion.2
  537.7 4.7 convert_add_fusion.2
  542.4 8.3 %convolution_add_fusion = f32[64,64,256]{2,1,0:T(8,128)} fusion(f32[64,64,256]{2,1,0:T(8,128)} %fusion.20, bf16[256,64,128]{2,0,1:T(8,128)(2,1)} %copy-done.2, f32[64,128,64]{2,1,0:T(8,128)} %get-tuple-element.212, f32[64]{0:T(128)S(1)} %copy-done.20), kind=kOutput, calls=%fused_computation.33 | convolution fusion | flops 270532608 | bytes 14680320 | tf_op jit(solution)/shard_map/kjhn,khnp->kjhp/dot_general | solution.py:186
  550.7 5.6 copy.157
  556.3 7.3 %add_convert_fusion = bf16[256,4096]{1,0:T(8,128)(2,1)} fusion(f32[256,4096]{1,0:T(8,128)} %get-tuple-element.334, f32[256,4096]{1,0:T(8,128)} %copy.156, f32[256,4096]{1,0:T(8,128)} %copy.157, f32[4096]{0:T(1024)S(1)} %mul.324), kind=kLoop, calls=%fused_computation.24 | loop fusion | flops 4194304 | bytes 14696448 | tf_op jit(solution)/shard_map/convert_element_type | solution.py:192
  (151 shorter events, 94.6 us)
Async XLA Ops:
  7.2 37.9 %copy-start = (bf16[256,2048]{1,0:T(8,128)(2,1)S(1)}, bf16[256,2048]{1,0:T(8,128)(2,1)}, u32[]{:S(2)}) copy-start(bf16[256,2048]{1,0:T(8,128)(2,1)} %param.29) | copy-start | bytes 3145732
  7.2 7.6 %copy-start.7 = (bf16[256,4096]{1,0:T(8,128)(2,1)S(1)}, bf16[256,4096]{1,0:T(8,128)(2,1)}, u32[]{:S(2)}) copy-start(bf16[256,4096]{1,0:T(8,128)(2,1)} %param.17) | copy-start | bytes 6291460
  7.2 106.1 %all-gather.10.cloned.1.call-start = ((), (), s32[]{:S(2)}) async-start(), calls=%async_computation.1 | async-start | bytes 18874368 | tf_op jit(solution)/shard_map/all_gather | solution.py:19
  10.7 0.6 copy-start.12
  11.9 9.7 %copy-start.23 = (f32[64]{0:T(128)}, f32[64]{0:T(128)S(1)}, u32[]{:S(2)}) copy-start(f32[64]{0:T(128)S(1)} %get-tuple-element.344) | copy-start | bytes 772
  17.7 5.8 %copy-start.3 = (f32[256,4096]{0,1:T(8,128)S(1)}, f32[256,4096]{0,1:T(8,128)}, u32[]{:S(2)}) copy-start(f32[256,4096]{0,1:T(8,128)} %copy.131) | copy-start | bytes 12582916
  21.6 1.9 copy-start.2
  23.5 3.2 copy-start.11
  23.5 3.3 copy-start.13
  23.5 3.4 copy-start.25
  23.5 3.6 copy-start.17
  23.5 4.2 copy-start.10
  25.8 199.6 %all-gather.8.cloned.1.call-start = ((), (), s32[]{:S(2)}) async-start(), calls=%async_computation | async-start | bytes 16908288 | tf_op jit(solution)/shard_map/all_gather | solution.py:158
  26.6 400.5 %all-reduce.3.cloned.1.call-start = ((), (), s32[]{:S(2)}) async-start(), calls=%async_computation.3 | async-start | bytes 3145728 | tf_op jit(solution)/shard_map/psum | solution.py:193
  28.1 5.7 copy-start.22
  28.1 16.9 %copy-start.16 = (bf16[64,2048]{1,0:T(8,128)(2,1)S(1)}, bf16[64,2048]{1,0:T(8,128)(2,1)}, u32[]{:S(2)}) copy-start(bf16[64,2048]{1,0:T(8,128)(2,1)} %param.27) | copy-start | bytes 786436
  193.4 5.8 %copy-start.1 = (bf16[64,256,256]{2,1,0:T(8,128)(2,1)S(1)}, bf16[64,256,256]{2,1,0:T(8,128)(2,1)}, u32[]{:S(2)}) copy-start(bf16[64,256,256]{2,1,0:T(8,128)(2,1)} %fusion.1) | copy-start | bytes 25165828
  207.3 5.8 %copy-start.8 = (bf16[256,4096]{1,0:T(8,128)(2,1)S(1)}, bf16[256,4096]{1,0:T(8,128)(2,1)}, u32[]{:S(2)}) copy-start(bf16[256,4096]{1,0:T(8,128)(2,1)} %param.17) | copy-start | bytes 6291460
  225.4 8.2 %copy-start.9 = (bf16[64,4096]{1,0:T(8,128)(2,1)S(1)}, bf16[64,4096]{1,0:T(8,128)(2,1)}, u32[]{:S(2)}) copy-start(bf16[64,4096]{1,0:T(8,128)(2,1)} %param.26) | copy-start | bytes 1572868
  225.4 8.2 %copy-start.14 = (bf16[256,64]{0,1:T(8,128)(2,1)S(1)}, bf16[256,64]{0,1:T(8,128)(2,1)}, u32[]{:S(2)}) copy-start(bf16[256,64]{0,1:T(8,128)(2,1)} %convolution_convert_fusion) | copy-start | bytes 98308
  236.3 6.0 %copy-start.19 = (f32[4,1024]{1,0:T(4,128)S(1)}, f32[4,1024]{1,0:T(4,128)}, u32[]{:S(2)}) copy-start(f32[4,1024]{1,0:T(4,128)} %mul.342) | copy-start | bytes 49156
  260.3 4.8 copy-start.6
  260.3 4.8 copy-start.18
  260.9 4.2 copy-start.4
  261.0 4.2 copy-start.5
  265.2 6.4 %copy-start.15 = (bf16[256,64]{0,1:T(8,128)(2,1)S(1)}, bf16[256,64]{0,1:T(8,128)(2,1)}, u32[]{:S(2)}) copy-start(bf16[256,64]{0,1:T(8,128)(2,1)} %convolution_convert_fusion) | copy-start | bytes 98308
  276.2 200.8 %all-gather.12.cloned.1.call-start = ((), (), s32[]{:S(2)}) async-start(), calls=%async_computation.2 | async-start | bytes 9437184 | tf_op jit(solution)/shard_map/all_gather | solution.py:36
  276.3 7.1 %copy-start.24 = (f32[64]{0:T(128)S(1)}, f32[64]{0:T(128)}, u32[]{:S(2)}) copy-start(f32[64]{0:T(128)} %copy-done.23) | copy-start | bytes 772
  289.9 5.7 copy-start.21
  479.5 62.9 %copy-start.20 = (f32[64]{0:T(128)S(1)}, f32[64]{0:T(128)}, u32[]{:S(2)}) copy-start(f32[64]{0:T(128)} %get-tuple-element.343) | copy-start | bytes 772
Sparse Core Ops, SparseCore 0:
  25.9 87.3 all-gather.9
  116.4 80.5 all-gather.7
  276.3 150.7 all-reduce.2
  429.2 47.7 all-gather.11
where the time goes:
time: 576 us; the launch traced here: 570 us
  waiting for transfers between devices  225 us (39%)
  local copies, waits for them, and re-layouts  132 us (23%)
  other arithmetic  127 us (22%)
  matrix products  49.5 us (9%)
  blocking collectives  20.2 us (4%)
  between operations  15.8 us (3%)
    psum x1, waiting for transfers between devices, on_device(): down_total, up_total = lax.psum((down_portion, up_portion), ('dp', 'ctx'))  116 us
    all_gather x1, waiting for transfers between devices, entering(): pieces = jax.tree.map(lambda part: lax.all_gather(part, axis), value)  67.2 us
    select_n x7, other arithmetic, lap(): jnp.where(position < mine, new, old)  43 us
    all_gather x1, waiting for transfers between devices, carried_in(): lax.all_gather(a.astype(kind), axis)  41.6 us
    add x7, other arithmetic, combine(): earlier[1] * later[0][:, None, None] + later[1]  32.7 us
    dynamic_slice x14, local copies, waits for them, and re-layouts, lap(): longer = join(running, jax.tree.map(lambda part: part[position], pieces))  32.2 us
    dynamic_slice x14, local copies, waits for them, and re-layouts, one(): lax.dynamic_index_in_dim(a, source, 0, False).astype(own.dtype)  30 us
    unnamed x58, local copies, waits for them, and re-layouts  19.1 us
  transfers between devices with their start and end apart: 4, of which 3 were waited for; matrix products, arithmetic and copies ran while one was open for 27% of the time, Pallas kernels for 0%

commit v1 on v0

--- a/solution.py
+++ b/solution.py
@@ -12,6 +12,11 @@
 EPS_NORM = 1e-05
 CLIP_EPSILON = 1e-06
 ADAPTER_SCALE = 2.0
+
+
+def axis_by_axis(x, one_2, other):
+    partial = lax.psum(x, one_2)
+    return lax.psum(partial, other)
 
 
 def entering(value, axis, join, neutral):
@@ -190,7 +195,7 @@
         row_count, H, P_SIZE
     ) + skip_coefficients[None, :, None] * d_ssd.reshape(row_count, H, P_SIZE)
     input_gradient = grad_heads.reshape(row_count, INNER_CHANNELS).astype(jnp.bfloat16)
-    down_total, up_total = lax.psum((down_portion, up_portion), ("dp", "ctx"))
+    down_total, up_total = axis_by_axis((down_portion, up_portion), "ctx", "dp")
     down_root_mean = jnp.sqrt(jnp.mean(down_total * down_total) + CLIP_EPSILON)
     up_root_mean = jnp.sqrt(jnp.mean(up_total * up_total) + CLIP_EPSILON)
     device_total = lax.axis_size(("dp", "ctx"))

time: 576 us -> 583 us (1.012)
  waiting for transfers between devices: 225 us -> 233 us
    psum x1 -> x2, waiting for transfers between devices: 116 us -> 122 us  [the longest x1 64.7 us: axis_by_axis(): partial = lax.psum(x, one_2)]
  transfers between devices with their start and end apart: 4 -> 5, of which waited for: 3 -> 4; matrix products, arithmetic and copies ran while one was open for 27% -> 26% of each run, Pallas kernels for 0% -> 0%
where the time goes in v1:
time: 583 us; the launch traced here: 578 us
  waiting for transfers between devices  233 us (40%)
  local copies, waits for them, and re-layouts  132 us (23%)
  other arithmetic  128 us (22%)
  matrix products  49.4 us (8%)
  blocking collectives  19.3 us (3%)
  between operations  15.9 us (3%)
    all_gather x1, waiting for transfers between devices, entering(): pieces = jax.tree.map(lambda part: lax.all_gather(part, axis), value)  67.3 us
    psum x1, waiting for transfers between devices, axis_by_axis(): partial = lax.psum(x, one_2)  64.7 us
    psum x1, waiting for transfers between devices, axis_by_axis(): return lax.psum(partial, other)  57.6 us
    all_gather x1, waiting for transfers between devices, carried_in(): lax.all_gather(a.astype(kind), axis)  42.9 us
    select_n x7, other arithmetic, lap(): jnp.where(position < mine, new, old)  42.9 us
    add x7, other arithmetic, combine(): earlier[1] * later[0][:, None, None] + later[1]  32.8 us
    dynamic_slice x14, local copies, waits for them, and re-layouts, lap(): longer = join(running, jax.tree.map(lambda part: part[position], pieces))  32.3 us
    dynamic_slice x14, local copies, waits for them, and re-layouts, one(): lax.dynamic_index_in_dim(a, source, 0, False).astype(own.dtype)  30 us
  transfers between devices with their start and end apart: 5, of which 4 were waited for; matrix products, arithmetic and copies ran while one was open for 26% of the time, Pallas kernels for 0%

profile of v1, /device:TPU:0, one launch (start us, length us, event | category | flops | bytes accessed | tf_op | source)
XLA Modules:
  0.0 577.6 jit_solution(285175758854780803)
XLA Ops:
  14.9 3.0 copy.131
  17.9 3.8 fusion.3
  28.2 5.7 fusion.1
  33.9 11.1 %all-gather = f32[8,1,64]{2,1,0:T(1,128)} all-gather(f32[1,1,64]{2,1,0:T(1,128)S(1)} %copy-done.22), channel_id=2, replica_groups=mesh['dp'=16,'ctx'=8] {'ctx'}, dimensions={0}, use_global_device_ids=true | all-gather | bytes 2304 | tf_op jit(solution)/shard_map/all_gather | solution.py:24
  46.1 67.3 %all-gather.10.cloned.1.call-done = f32[512,128,64]{1,2,0:T(8,128)} async-done(((f32[64,128,64]{1,2,0:T(8,128)}), f32[512,128,64]{1,2,0:T(8,128)}) %all-gather.10.cloned.1.call-update) | async-done | bytes 16777232 | tf_op jit(solution)/shard_map/all_gather | solution.py:24
  113.4 80.0 %while.19 = (s32[]{:T(128)}, f32[64,128,64]{2,1,0:T(8,128)}, s32[]{:T(128)}, f32[8,64]{1,0:T(8,128)}, f32[8,64,128,64]{2,3,1,0:T(8,128)}, /*index=5*/s32[]{:T(128)}, s32[]{:T(128)}) while((s32[]{:T(128)}, f32[64,128,64]{2,1,0:T(8,128)}, s32[]{:T(128)}, f32[8,64]{1,0:T(8,128)}, f32[8,64,128,64]{2,3,1,0:T(8,128)}, ...), condition=%wide.region_3.4_spmd.clone, body=%wide.region_2.3_spmd.clone.sunk | while | flops 2097156 | bytes 14680945 | solution.py:33
  118.6 4.8 fusion.43
  128.7 6.1 %fusion.43 = f32[64,128,64]{2,1,0:T(8,128)} fusion(f32[1,64,128,64]{3,2,1,0:T(8,128)} %copy.195, f32[64,128,64]{2,1,0:T(8,128)} %get-tuple-element.420, f32[64]{0:T(128)S(1)} %dynamic-slice_bitcast_fusion.2, pred[]{:T(512)S(6)} %compare.3, pred[]{:T(512)S(6)} %lt.51), kind=kLoop, calls=%fused_computation.4.clone.1 | loop fusion | flops 2097152 | bytes 6291714 | tf_op jit(solution)/shard_map/while/body/eval_jaxpr/jit(_where)/select_n | solution.py:31
  140.0 6.1 %fusion.43 = f32[64,128,64]{2,1,0:T(8,128)} fusion(f32[1,64,128,64]{3,2,1,0:T(8,128)} %copy.195, f32[64,128,64]{2,1,0:T(8,128)} %get-tuple-element.420, f32[64]{0:T(128)S(1)} %dynamic-slice_bitcast_fusion.2, pred[]{:T(512)S(6)} %compare.3, pred[]{:T(512)S(6)} %lt.51), kind=kLoop, calls=%fused_computation.4.clone.1 | loop fusion | flops 2097152 | bytes 6291714 | tf_op jit(solution)/shard_map/while/body/eval_jaxpr/jit(_where)/select_n | solution.py:31
  151.3 6.3 %fusion.43 = f32[64,128,64]{2,1,0:T(8,128)} fusion(f32[1,64,128,64]{3,2,1,0:T(8,128)} %copy.195, f32[64,128,64]{2,1,0:T(8,128)} %get-tuple-element.420, f32[64]{0:T(128)S(1)} %dynamic-slice_bitcast_fusion.2, pred[]{:T(512)S(6)} %compare.3, pred[]{:T(512)S(6)} %lt.51), kind=kLoop, calls=%fused_computation.4.clone.1 | loop fusion | flops 2097152 | bytes 6291714 | tf_op jit(solution)/shard_map/while/body/eval_jaxpr/jit(_where)/select_n | solution.py:31
  162.9 6.1 %fusion.43 = f32[64,128,64]{2,1,0:T(8,128)} fusion(f32[1,64,128,64]{3,2,1,0:T(8,128)} %copy.195, f32[64,128,64]{2,1,0:T(8,128)} %get-tuple-element.420, f32[64]{0:T(128)S(1)} %dynamic-slice_bitcast_fusion.2, pred[]{:T(512)S(6)} %compare.3, pred[]{:T(512)S(6)} %lt.51), kind=kLoop, calls=%fused_computation.4.clone.1 | loop fusion | flops 2097152 | bytes 6291714 | tf_op jit(solution)/shard_map/while/body/eval_jaxpr/jit(_where)/select_n | solution.py:31
  174.8 6.8 %fusion.43 = f32[64,128,64]{2,1,0:T(8,128)} fusion(f32[1,64,128,64]{3,2,1,0:T(8,128)} %copy.195, f32[64,128,64]{2,1,0:T(8,128)} %get-tuple-element.420, f32[64]{0:T(128)S(1)} %dynamic-slice_bitcast_fusion.2, pred[]{:T(512)S(6)} %compare.3, pred[]{:T(512)S(6)} %lt.51), kind=kLoop, calls=%fused_computation.4.clone.1 | loop fusion | flops 2097152 | bytes 6291714 | tf_op jit(solution)/shard_map/while/body/eval_jaxpr/jit(_where)/select_n | solution.py:31
  183.3 2.8 copy.195
  186.9 6.5 %fusion.43 = f32[64,128,64]{2,1,0:T(8,128)} fusion(f32[1,64,128,64]{3,2,1,0:T(8,128)} %copy.195, f32[64,128,64]{2,1,0:T(8,128)} %get-tuple-element.420, f32[64]{0:T(128)S(1)} %dynamic-slice_bitcast_fusion.2, pred[]{:T(512)S(6)} %compare.3, pred[]{:T(512)S(6)} %lt.51), kind=kLoop, calls=%fused_computation.4.clone.1 | loop fusion | flops 2097152 | bytes 6291714 | tf_op jit(solution)/shard_map/while/body/eval_jaxpr/jit(_where)/select_n | solution.py:31
  193.4 2.9 multiply_convert_fusion.2
  196.3 2.9 fusion.15
  199.2 8.2 %fusion.8 = f32[1,256,64,64]{1,3,2,0:T(8,128)} fusion(f32[4,16,64,256]{3,2,1,0:T(8,128)} %fusion.15, bf16[64,256,256]{2,1,0:T(8,128)(2,1)S(1)} %copy-done.1, f32[256,64]{0,1:T(8,128)S(1)} %copy.139, f32[256,64,64]{0,2,1:T(8,128)} %bitcast.133, f32[256,64]{0,1:T(8,128)S(1)} %get-tuple-element.340), kind=kOutput, calls=%fused_computation.22 | convolution fusion | flops 541065216 | bytes 21102592 | tf_op jit(solution)/shard_map/khij,kjhp->kihp/dot_general | solution.py:112
  207.4 5.8 copy.145
  213.2 6.3 %add_multiply_fusion = f32[256,4096]{1,0:T(8,128)} fusion(f32[256,4096]{1,0:T(8,128)} %copy.145, f32[4096]{0:T(1024)S(1)} %mul.324, bf16[256,4096]{1,0:T(8,128)(2,1)} %param.18, bf16[256,4096]{1,0:T(8,128)(2,1)S(1)} %copy-done.8), kind=kLoop, calls=%fused_computation.29 | loop fusion | flops 9437184 | bytes 12599296 | tf_op jit(solution)/shard_map/mul | solution.py:141
  219.4 6.0 %reshape.335 = f32[256,4,1024]{2,1,0:T(4,128)} reshape(f32[256,4096]{1,0:T(8,128)} %add_multiply_fusion) | data formatting | bytes 8388608 | tf_op jit(solution)/shard_map/reshape | solution.py:141
  225.4 8.2 %fusion.19 = f32[256,4096]{1,0:T(8,128)S(1)} fusion(bf16[256,2048]{1,0:T(8,128)(2,1)S(1)} %copy-done, bf16[2048,4096]{1,0:T(8,128)(2,1)} %all-gather.8.cloned.1.call-done), kind=kOutput, calls=%fused_computation.71 | convolution fusion | flops 4294967296 | bytes 22020096 | tf_op jit(solution)/shard_map/dot_general | solution.py:164
  236.3 6.0 %reshape.336 = f32[256,4,1024]{2,1,0:T(4,128)} reshape(f32[256,4096]{1,0:T(8,128)} %fusion.4) | data formatting | bytes 8388608 | tf_op jit(solution)/shard_map/reshape | solution.py:167
  242.3 4.8 multiply_reduce_fusion.1
  247.8 5.8 copy.175
  254.4 5.8 %copy.174 = f32[32,8,4,1024]{3,1,2,0:T(8,128)} copy(f32[32,8,4,1024]{3,2,1,0:T(4,128)S(1)} %bitcast.143) | data formatting | bytes 8388608
  261.0 4.2 copy.173
  265.2 6.4 %fusion.18 = (bf16[256,4096]{1,0:T(8,128)(2,1)}, f32[256,4096]{1,0:T(8,128)}, bf16[256,4096]{1,0:T(8,128)(2,1)S(1)}) fusion(bf16[256,4096]{1,0:T(8,128)(2,1)} %param.18, f32[256,4096]{1,0:T(8,128)S(1)} %bitcast.137, f32[256,4096]{1,0:T(8,128)S(1)} %copy-done.4, f32[256,4096]{1,0:T(8,128)} %bitcast.138, f32[256,4096]{1,0:T(8,128)S(1)} %bitcast.139, ...), kind=kLoop, calls=%fused_computation.70 | loop fusion | flops 15728640 | bytes 31473664 | tf_op jit(solution)/shard_map/convert_element_type | solution.py:172
  273.1 3.1 convolution_multiply_fusion.2
  276.3 64.7 %all-reduce.7.cloned.1.call-done = (f32[64,4096]{1,0:T(8,128)}, f32[64,2048]{1,0:T(8,128)}) async-done(((f32[64,4096]{1,0:T(8,128)}, f32[64,2048]{1,0:T(8,128)}), (f32[64,4096]{1,0:T(8,128)}, f32[64,2048]{1,0:T(8,128)})) %all-reduce.7.cloned.1.call-update) | async-done | bytes 1572880 | tf_op jit(solution)/shard_map/psum | solution.py:18
  341.1 3.8 fusion.2
  344.9 3.3 copy.151
  348.2 4.1 add_convert_fusion.1
  354.6 5.6 copy.156
  360.2 8.2 %all-gather.3 = bf16[8,1,64]{2,1,0:T(2,128)(2,1)S(1)} all-gather(bf16[1,1,64]{2,1,0:T(2,128)(2,1)S(1)} %copy-done.21), channel_id=5, replica_groups=mesh['dp'=16,'ctx'=8] {'ctx'}, dimensions={0}, use_global_device_ids=true | all-gather | bytes 1152 | tf_op jit(solution)/shard_map/all_gather | solution.py:41
  368.4 6.9 %fusion.20 = f32[64,64,256]{2,1,0:T(8,128)} fusion(bf16[256,64,64]{0,2,1:T(8,128)(2,1)S(1)} %bitcast.136, bf16[64,256,256]{2,1,0:T(8,128)(2,1)} %fusion.1), kind=kOutput, calls=%fused_computation.72 | convolution fusion | flops 536870912 | bytes 14680064 | tf_op jit(solution)/shard_map/khij,kihp->kjhp/dot_general | solution.py:173
  375.3 57.6 %all-reduce.5.cloned.1.call-done = (f32[64,4096]{1,0:T(8,128)}, f32[64,2048]{1,0:T(8,128)}) async-done(((f32[64,4096]{1,0:T(8,128)}, f32[64,2048]{1,0:T(8,128)}), (f32[64,4096]{1,0:T(8,128)}, f32[64,2048]{1,0:T(8,128)})) %all-reduce.5.cloned.1.call-update) | async-done | bytes 1572880 | tf_op jit(solution)/shard_map/psum | solution.py:19
  441.2 42.9 %all-gather.12.cloned.1.call-done = bf16[512,128,64]{1,2,0:T(8,128)(2,1)} async-done(((bf16[64,128,64]{1,2,0:T(8,128)(2,1)}), bf16[512,128,64]{1,2,0:T(8,128)(2,1)}) %all-gather.12.cloned.1.call-update) | async-done | bytes 8388624 | tf_op jit(solution)/shard_map/all_gather | solution.py:41
  486.7 62.9 %while.18 = (s32[]{:T(128)}, f32[64,128,64]{2,1,0:T(8,128)}, s32[]{:T(128)}, bf16[8,64]{1,0:T(8,128)(2,1)S(1)}, bf16[8,64,128,64]{2,3,1,0:T(8,128)(2,1)}, /*index=5*/s32[]{:T(128)}, s32[]{:T(128)}, s32[]{:T(128)}, s32[]{:T(128)}) while((s32[]{:T(128)}, f32[64,128,64]{2,1,0:T(8,128)}, s32[]{:T(128)}, bf16[8,64]{1,0:T(8,128)(2,1)S(1)}, ...), condition=%wide.region_7.8_spmd, body=%wide.region_6.7_spmd.sunk | while | flops 1572934 | bytes 9437979 | solution.py:56
  491.0 4.7 convert_add_fusion.2
  500.0 4.7 convert_add_fusion.2
  509.0 4.7 convert_add_fusion.2
  518.0 4.7 convert_add_fusion.2
  527.0 4.7 convert_add_fusion.2
  536.0 4.7 convert_add_fusion.2
  545.0 4.7 convert_add_fusion.2
  549.6 8.3 %convolution_add_fusion = f32[64,64,256]{2,1,0:T(8,128)} fusion(f32[64,64,256]{2,1,0:T(8,128)} %fusion.20, bf16[256,64,128]{2,0,1:T(8,128)(2,1)} %copy-done.2, f32[64,128,64]{2,1,0:T(8,128)} %get-tuple-element.212, f32[64]{0:T(128)S(1)} %copy-done.20), kind=kOutput, calls=%fused_computation.33 | convolution fusion | flops 270532608 | bytes 14680320 | tf_op jit(solution)/shard_map/kjhn,khnp->kjhp/dot_general | solution.py:191
  558.0 5.6 copy.157
  563.6 7.3 %add_convert_fusion = bf16[256,4096]{1,0:T(8,128)(2,1)} fusion(f32[256,4096]{1,0:T(8,128)} %get-tuple-element.336, f32[256,4096]{1,0:T(8,128)} %copy.156, f32[256,4096]{1,0:T(8,128)} %copy.157, f32[4096]{0:T(1024)S(1)} %mul.324), kind=kLoop, calls=%fused_computation.24 | loop fusion | flops 4194304 | bytes 14696448 | tf_op jit(solution)/shard_map/convert_element_type | solution.py:197
  (154 shorter events, 97.6 us)
Async XLA Ops:
  7.2 37.9 %copy-start = (bf16[256,2048]{1,0:T(8,128)(2,1)S(1)}, bf16[256,2048]{1,0:T(8,128)(2,1)}, u32[]{:S(2)}) copy-start(bf16[256,2048]{1,0:T(8,128)(2,1)} %param.29) | copy-start | bytes 3145732
  7.2 7.7 %copy-start.7 = (bf16[256,4096]{1,0:T(8,128)(2,1)S(1)}, bf16[256,4096]{1,0:T(8,128)(2,1)}, u32[]{:S(2)}) copy-start(bf16[256,4096]{1,0:T(8,128)(2,1)} %param.17) | copy-start | bytes 6291460
  7.2 106.2 %all-gather.10.cloned.1.call-start = ((), (), s32[]{:S(2)}) async-start(), calls=%async_computation.1 | async-start | bytes 18874368 | tf_op jit(solution)/shard_map/all_gather | solution.py:24
  10.7 0.6 copy-start.12
  12.0 9.7 %copy-start.23 = (f32[64]{0:T(128)}, f32[64]{0:T(128)S(1)}, u32[]{:S(2)}) copy-start(f32[64]{0:T(128)S(1)} %get-tuple-element.346) | copy-start | bytes 772
  17.9 5.8 %copy-start.3 = (f32[256,4096]{0,1:T(8,128)S(1)}, f32[256,4096]{0,1:T(8,128)}, u32[]{:S(2)}) copy-start(f32[256,4096]{0,1:T(8,128)} %copy.131) | copy-start | bytes 12582916
  21.7 1.9 copy-start.2
  23.6 3.1 copy-start.11
  23.6 3.3 copy-start.13
  23.6 3.4 copy-start.25
  23.6 3.6 copy-start.17
  23.7 4.2 copy-start.10
  25.9 199.5 %all-gather.8.cloned.1.call-start = ((), (), s32[]{:S(2)}) async-start(), calls=%async_computation | async-start | bytes 16908288 | tf_op jit(solution)/shard_map/all_gather | solution.py:163
  26.7 314.3 %all-reduce.7.cloned.1.call-start = ((), (), s32[]{:S(2)}) async-start(), calls=%async_computation.4 | async-start | bytes 3145728 | tf_op jit(solution)/shard_map/psum | solution.py:18
  28.2 5.7 copy-start.22
  28.2 16.8 %copy-start.16 = (bf16[64,2048]{1,0:T(8,128)(2,1)S(1)}, bf16[64,2048]{1,0:T(8,128)(2,1)}, u32[]{:S(2)}) copy-start(bf16[64,2048]{1,0:T(8,128)(2,1)} %param.27) | copy-start | bytes 786436
  193.4 5.8 %copy-start.1 = (bf16[64,256,256]{2,1,0:T(8,128)(2,1)S(1)}, bf16[64,256,256]{2,1,0:T(8,128)(2,1)}, u32[]{:S(2)}) copy-start(bf16[64,256,256]{2,1,0:T(8,128)(2,1)} %fusion.1) | copy-start | bytes 25165828
  207.4 5.8 copy-start.8
  225.4 8.2 %copy-start.9 = (bf16[64,4096]{1,0:T(8,128)(2,1)S(1)}, bf16[64,4096]{1,0:T(8,128)(2,1)}, u32[]{:S(2)}) copy-start(bf16[64,4096]{1,0:T(8,128)(2,1)} %param.26) | copy-start | bytes 1572868
  225.4 8.2 %copy-start.14 = (bf16[256,64]{0,1:T(8,128)(2,1)S(1)}, bf16[256,64]{0,1:T(8,128)(2,1)}, u32[]{:S(2)}) copy-start(bf16[256,64]{0,1:T(8,128)(2,1)} %convolution_convert_fusion) | copy-start | bytes 98308
  236.3 6.0 %copy-start.19 = (f32[4,1024]{1,0:T(4,128)S(1)}, f32[4,1024]{1,0:T(4,128)}, u32[]{:S(2)}) copy-start(f32[4,1024]{1,0:T(4,128)} %mul.342) | copy-start | bytes 49156
  260.3 4.8 copy-start.6
  260.3 4.8 copy-start.18
  261.0 4.2 copy-start.4
  261.0 4.2 copy-start.5
  265.2 6.4 %copy-start.15 = (bf16[256,64]{0,1:T(8,128)(2,1)S(1)}, bf16[256,64]{0,1:T(8,128)(2,1)}, u32[]{:S(2)}) copy-start(bf16[256,64]{0,1:T(8,128)(2,1)} %convolution_convert_fusion) | copy-start | bytes 98308
  276.2 156.7 %all-reduce.5.cloned.1.call-start = ((), (), s32[]{:S(2)}) async-start(), calls=%async_computation.3 | async-start | bytes 3145728 | tf_op jit(solution)/shard_map/psum | solution.py:19
  341.0 143.2 %all-gather.12.cloned.1.call-start = ((), (), s32[]{:S(2)}) async-start(), calls=%async_computation.2 | async-start | bytes 9437184 | tf_op jit(solution)/shard_map/all_gather | solution.py:41
  341.1 7.1 %copy-start.24 = (f32[64]{0:T(128)S(1)}, f32[64]{0:T(128)}, u32[]{:S(2)}) copy-start(f32[64]{0:T(128)} %copy-done.23) | copy-start | bytes 772
  354.6 5.6 copy-start.21
  486.7 63.0 %copy-start.20 = (f32[64]{0:T(128)S(1)}, f32[64]{0:T(128)}, u32[]{:S(2)}) copy-start(f32[64]{0:T(128)} %get-tuple-element.345) | copy-start | bytes 772
Sparse Core Ops, SparseCore 0:
  26.0 87.3 all-gather.9
  116.6 80.5 all-gather.7
  276.3 64.5 all-reduce.6
  344.2 88.6 all-reduce.4
  435.1 49.0 all-gather.11
